TPU v7x, 32 devices: a whole 2x2x4 slice. The times are simulated.
32 devices in a mesh: dp: 16 (over z, y, core), tensor: 2 (over x).
Axes of the slice: x: 2, y: 2, z: 4, core: 2. Of those that a mesh axis runs over, the one named last changes fastest.
Arguments:
- layer_input: float32 [8192, 1024], P(('dp', 'tensor')), may hold values from -6 to 6
- segment_ids: int32 [16, 512], P('dp'), may hold values from 0 to 3, never falling along the last dimension, each value on 1 to 256 neighbouring positions
- norm1_gain: bfloat16 [1024], P('dp'), may hold values from 0.25 to 1.75
- norm1_shift: bfloat16 [1024], P('dp'), may hold values from -3 to 3
- qkv_weight: bfloat16 [1024, 3072], P('dp', 'tensor'), may hold values from -1 to 1
- qkv_bias: bfloat16 [2048], P(('tensor', 'dp')), may hold values from -3 to 3
- dense_weight: bfloat16 [1024, 1024], P('dp', 'tensor'), may hold values from -0.75 to 0.75
- dense_bias: bfloat16 [1024], P('dp'), may hold values from -3 to 3
- norm2_gain: bfloat16 [1024], P('dp'), may hold values from 0.25 to 1.75
- norm2_shift: bfloat16 [1024], P('dp'), may hold values from -3 to 3
- inner_weight: bfloat16 [1024, 4096], P('dp', 'tensor'), may hold values from -0.1875 to 0.1875
- inner_bias: bfloat16 [4096], P(('tensor', 'dp')), may hold values from -3 to 3
- outer_weight: bfloat16 [1024, 4096], P('dp', 'tensor'), may hold values from -0.1875 to 0.1875
- outer_bias: bfloat16 [1024], P('dp'), may hold values from -3 to 3
- out_cotangent: float32 [8192, 1024], P(('dp', 'tensor')), may hold values from -6 to 6
Outputs:
- layer_output: float32 [8192, 1024], P(('dp', 'tensor'))
- input_grad: float32 [8192, 1024], P(('dp', 'tensor'))
- norm1_gain_grad: float32 [1024], P('dp')
- norm1_shift_grad: float32 [1024], P('dp')
- qkv_weight_grad: float32 [1024, 3072], P('dp', 'tensor')
- qkv_bias_grad: float32 [2048], P(('tensor', 'dp'))
- dense_weight_grad: float32 [1024, 1024], P('dp', 'tensor')
- dense_bias_grad: float32 [1024], P('dp')
- norm2_gain_grad: float32 [1024], P('dp')
- norm2_shift_grad: float32 [1024], P('dp')
- inner_weight_grad: float32 [1024, 4096], P('dp', 'tensor')
- inner_bias_grad: float32 [4096], P(('tensor', 'dp'))
- outer_weight_grad: float32 [1024, 4096], P('dp', 'tensor')
- outer_bias_grad: float32 [1024], P('dp')
Inputs may be any that keep to these rules, and one draw needn't show every extreme that they name: `segment_ids`: along each row the ids never fall; each segment spans 1 to 256 positions, and one spans exactly 256.
All inputs are finite; a program needn't handle non-finite values.
Results may differ from a plain program's by a relative error of at most 0.024.
Values may be sent and summed in bfloat16 or wider, within the bound.
No kernel may reach another device: no remote copies, remote signals or barrier semaphores. Data moves between devices by JAX's collectives and lax.ppermute only.
A program may use at most 128 MiB of HBM per device.

v0:
```python
import jax
import jax.numpy as jnp
from jax import lax
from jax.sharding import PartitionSpec as P

H = 16
HD = 64
EPSILON = 1e-05
GELU_C = 0.7978845608028654
GELU_K = 0.044715


def layer_norm(row_data, gain, shift):
    row_mean = jnp.mean(row_data, axis=-1, keepdims=True)
    centered = row_data - row_mean
    row_var = jnp.mean(centered * centered, axis=-1, keepdims=True)
    inv_std = lax.rsqrt(row_var + EPSILON)
    normed = centered * inv_std
    return (normed * gain.astype(jnp.float32) + shift.astype(jnp.float32), normed, inv_std)


def norm_back(grad_out, normed, inv_std, gain):
    scaled = grad_out * gain.astype(jnp.float32)
    mean_grad = jnp.mean(scaled, axis=-1, keepdims=True)
    mean_cross = jnp.mean(scaled * normed, axis=-1, keepdims=True)
    return inv_std * (scaled - mean_grad - normed * mean_cross)


def gelu_parts(pre_act):
    cubed_term = pre_act * pre_act * pre_act
    tangent = jnp.tanh(GELU_C * (pre_act + GELU_K * cubed_term))
    result = 0.5 * pre_act * (1.0 + tangent)
    derivative = 0.5 * (1.0 + tangent) + 0.5 * pre_act * (1.0 - tangent * tangent) * GELU_C * (
        1.0 + 3.0 * GELU_K * pre_act * pre_act
    )
    return (result, derivative)


def rows_product(left, right):
    return lax.dot_general(
        left, right, (((0,), (0,)), ((), ())), preferred_element_type=jnp.float32
    )


def cross_product(left, right):
    return lax.dot_general(
        left, right, (((1,), (1,)), ((), ())), preferred_element_type=jnp.float32
    )


def block_scores(query_block, key_rows, segment_row, head_slopes):
    block_len = query_block.shape[0]
    scores = jnp.einsum(
        "bhe,the->hbt", query_block, key_rows, preferred_element_type=jnp.float32
    ) * HD ** (-0.5)
    row_pos = jnp.arange(block_len, dtype=jnp.int32)
    col_pos = jnp.arange(key_rows.shape[0], dtype=jnp.int32)
    allowed = (col_pos[None, :] <= row_pos[:, None]) & (
        segment_row[:, None] == segment_row[None, :]
    )
    distance = (row_pos[:, None] - col_pos[None, :]).astype(jnp.float32)
    scores = scores - head_slopes[:, None, None] * distance[None]
    return jnp.where(allowed[None], scores, -1e30)


def attend_forward(query_rows, key_rows, value_rows, segment_row, head_slopes):
    scores = block_scores(query_rows, key_rows, segment_row, head_slopes)
    row_max = jnp.max(scores, axis=-1, keepdims=True)
    log_total = row_max + jnp.log(jnp.sum(jnp.exp(scores - row_max), axis=-1, keepdims=True))
    attn_probs = jnp.exp(scores - log_total).astype(jnp.bfloat16)
    context = jnp.einsum("hbt,the->bhe", attn_probs, value_rows, preferred_element_type=jnp.float32)
    outputs = context.astype(jnp.bfloat16)
    return (outputs, log_total)


def attend_backward(
    query_rows, key_rows, value_rows, context, context_grad, log_total, segment_row, head_slopes
):
    scale = HD ** (-0.5)
    scores = block_scores(query_rows, key_rows, segment_row, head_slopes)
    probs = jnp.exp(scores - log_total)
    probs_low = probs.astype(jnp.bfloat16)
    value_grad = jnp.einsum(
        "hbt,bhe->the", probs_low, context_grad, preferred_element_type=jnp.float32
    )
    prob_grad = jnp.einsum(
        "bhe,the->hbt", context_grad, value_rows, preferred_element_type=jnp.float32
    )
    delta = jnp.sum(context_grad.astype(jnp.float32) * context.astype(jnp.float32), axis=-1)
    score_grad = (probs * (prob_grad - jnp.transpose(delta)[:, :, None])).astype(jnp.bfloat16)
    query_parts = (
        jnp.einsum("hbt,the->bhe", score_grad, key_rows, preferred_element_type=jnp.float32) * scale
    )
    key_grad = (
        jnp.einsum("hbt,bhe->the", score_grad, query_rows, preferred_element_type=jnp.float32)
        * scale
    )
    return (query_parts, key_grad, value_grad)


def on_device(
    layer_input,
    segment_ids,
    norm1_gain,
    norm1_shift,
    qkv_weight,
    qkv_bias,
    dense_weight,
    dense_bias,
    norm2_gain,
    norm2_shift,
    inner_weight,
    inner_bias,
    outer_weight,
    outer_bias,
    out_cotangent,
):
    gathered = (
        lax.all_gather(norm1_gain, "dp", axis=0, tiled=True),
        lax.all_gather(norm1_shift, "dp", axis=0, tiled=True),
        lax.all_gather(qkv_weight, "dp", axis=0, tiled=True),
        lax.all_gather(qkv_bias, "dp", axis=0, tiled=True),
        lax.all_gather(dense_weight, "dp", axis=0, tiled=True),
        lax.all_gather(dense_bias, "dp", axis=0, tiled=True),
        lax.all_gather(norm2_gain, "dp", axis=0, tiled=True),
        lax.all_gather(norm2_shift, "dp", axis=0, tiled=True),
        lax.all_gather(inner_weight, "dp", axis=0, tiled=True),
        lax.all_gather(inner_bias, "dp", axis=0, tiled=True),
        lax.all_gather(outer_weight, "dp", axis=0, tiled=True),
        lax.all_gather(outer_bias, "dp", axis=0, tiled=True),
    )
    (
        gain_one,
        shift_one,
        qkv_full,
        qkv_bias_full,
        dense_full,
        dense_bias_full,
        gain_two,
        shift_two,
        inner_full,
        inner_bias_full,
        outer_full,
        outer_bias_full,
    ) = gathered
    local_heads = qkv_full.shape[1] // (3 * HD)
    head_index = lax.axis_index("tensor") * local_heads + jnp.arange(local_heads, dtype=jnp.int32)
    head_slopes = jnp.exp2(-8.0 * (head_index.astype(jnp.float32) + 1.0) / H)
    segment_row = segment_ids[0]
    bias_pairs = qkv_bias_full.astype(jnp.float32).reshape(local_heads, 2, HD)
    bias_three = jnp.stack(
        [bias_pairs[:, 0], jnp.zeros_like(bias_pairs[:, 0]), bias_pairs[:, 1]], axis=1
    ).reshape(-1)
    normed_one, hat_one, inv_one = layer_norm(layer_input, gain_one, shift_one)
    norm_rows = lax.all_gather(normed_one.astype(jnp.bfloat16), "tensor", axis=0, tiled=True)
    group_rows = norm_rows.shape[0]
    projected = (
        jnp.dot(norm_rows, qkv_full, preferred_element_type=jnp.float32) + bias_three
    ).astype(jnp.bfloat16)
    projected = projected.reshape(group_rows, local_heads, 3, HD)
    query_rows = projected[:, :, 0]
    key_rows = projected[:, :, 1]
    value_rows = projected[:, :, 2]
    context, log_total = attend_forward(query_rows, key_rows, value_rows, segment_row, head_slopes)
    context_flat = context.reshape(group_rows, local_heads * HD)
    attn_part = lax.psum_scatter(
        cross_product(context_flat, dense_full).astype(jnp.bfloat16),
        "tensor",
        scatter_dimension=0,
        tiled=True,
    ).astype(jnp.float32)
    middle = layer_input + attn_part + dense_bias_full.astype(jnp.float32)
    normed_two, hat_two, inv_two = layer_norm(middle, gain_two, shift_two)
    mid_rows = lax.all_gather(normed_two.astype(jnp.bfloat16), "tensor", axis=0, tiled=True)
    pre_act = jnp.dot(
        mid_rows, inner_full, preferred_element_type=jnp.float32
    ) + inner_bias_full.astype(jnp.float32)
    act_value, act_slope = gelu_parts(pre_act)
    act_low = act_value.astype(jnp.bfloat16)
    layer_output = (
        middle
        + lax.psum_scatter(
            cross_product(act_low, outer_full).astype(jnp.bfloat16),
            "tensor",
            scatter_dimension=0,
            tiled=True,
        ).astype(jnp.float32)
        + outer_bias_full.astype(jnp.float32)
    )
    back_set = (
        lax.all_gather(norm1_gain, "dp", axis=0, tiled=True),
        lax.all_gather(qkv_weight, "dp", axis=0, tiled=True),
        lax.all_gather(dense_weight, "dp", axis=0, tiled=True),
        lax.all_gather(norm2_gain, "dp", axis=0, tiled=True),
        lax.all_gather(inner_weight, "dp", axis=0, tiled=True),
        lax.all_gather(outer_weight, "dp", axis=0, tiled=True),
    )
    gain_back_one, qkv_back, dense_back, gain_back_two, inner_back, outer_back = back_set
    cot_rows = lax.all_gather(out_cotangent.astype(jnp.bfloat16), "tensor", axis=0, tiled=True)
    outer_grad = rows_product(cot_rows, act_low)
    pre_grad = jnp.dot(cot_rows, outer_back, preferred_element_type=jnp.float32) * act_slope
    inner_bias_grad = jnp.sum(pre_grad, axis=0)
    pre_low = pre_grad.astype(jnp.bfloat16)
    inner_grad = rows_product(mid_rows, pre_low)
    mid_grad = lax.psum_scatter(
        cross_product(pre_low, inner_back).astype(jnp.bfloat16),
        "tensor",
        scatter_dimension=0,
        tiled=True,
    ).astype(jnp.float32)
    gain_two_grad = jnp.sum(mid_grad * hat_two, axis=0)
    shift_two_grad = jnp.sum(mid_grad, axis=0)
    middle_grad = out_cotangent + norm_back(mid_grad, hat_two, inv_two, gain_back_two)
    dense_bias_grad = jnp.sum(middle_grad, axis=0)
    outer_bias_grad = jnp.sum(out_cotangent, axis=0)
    middle_rows = lax.all_gather(middle_grad.astype(jnp.bfloat16), "tensor", axis=0, tiled=True)
    dense_grad = rows_product(middle_rows, context_flat)
    context_grad = jnp.dot(middle_rows, dense_back, preferred_element_type=jnp.float32).astype(
        jnp.bfloat16
    )
    context_grad = context_grad.reshape(group_rows, local_heads, HD)
    query_grad, key_grad, value_grad = attend_backward(
        query_rows, key_rows, value_rows, context, context_grad, log_total, segment_row, head_slopes
    )
    qkv_grad = jnp.stack([query_grad, key_grad, value_grad], axis=2).reshape(
        group_rows, local_heads * 3 * HD
    )
    bias_sums = jnp.sum(qkv_grad, axis=0).reshape(local_heads, 3, HD)
    qkv_bias_grad = jnp.stack([bias_sums[:, 0], bias_sums[:, 2]], axis=1).reshape(-1)
    qkv_low = qkv_grad.astype(jnp.bfloat16)
    qkv_weight_grad = rows_product(norm_rows, qkv_low)
    first_grad = lax.psum_scatter(
        cross_product(qkv_low, qkv_back).astype(jnp.bfloat16),
        "tensor",
        scatter_dimension=0,
        tiled=True,
    ).astype(jnp.float32)
    gain_one_grad = jnp.sum(first_grad * hat_one, axis=0)
    shift_one_grad = jnp.sum(first_grad, axis=0)
    input_grad = middle_grad + norm_back(first_grad, hat_one, inv_one, gain_back_one)
    small_sums = lax.psum(
        (
            gain_one_grad,
            shift_one_grad,
            dense_bias_grad,
            gain_two_grad,
            shift_two_grad,
            outer_bias_grad,
        ),
        "tensor",
    )
    everything = (
        lax.psum_scatter(
            small_sums[0].astype(jnp.bfloat16), "dp", scatter_dimension=0, tiled=True
        ).astype(jnp.float32),
        lax.psum_scatter(
            small_sums[1].astype(jnp.bfloat16), "dp", scatter_dimension=0, tiled=True
        ).astype(jnp.float32),
        lax.psum_scatter(
            qkv_weight_grad.astype(jnp.bfloat16), "dp", scatter_dimension=0, tiled=True
        ).astype(jnp.float32),
        lax.psum_scatter(
            qkv_bias_grad.astype(jnp.bfloat16), "dp", scatter_dimension=0, tiled=True
        ).astype(jnp.float32),
        lax.psum_scatter(
            dense_grad.astype(jnp.bfloat16), "dp", scatter_dimension=0, tiled=True
        ).astype(jnp.float32),
        lax.psum_scatter(
            small_sums[2].astype(jnp.bfloat16), "dp", scatter_dimension=0, tiled=True
        ).astype(jnp.float32),
        lax.psum_scatter(
            small_sums[3].astype(jnp.bfloat16), "dp", scatter_dimension=0, tiled=True
        ).astype(jnp.float32),
        lax.psum_scatter(
            small_sums[4].astype(jnp.bfloat16), "dp", scatter_dimension=0, tiled=True
        ).astype(jnp.float32),
        lax.psum_scatter(
            inner_grad.astype(jnp.bfloat16), "dp", scatter_dimension=0, tiled=True
        ).astype(jnp.float32),
        lax.psum_scatter(
            inner_bias_grad.astype(jnp.bfloat16), "dp", scatter_dimension=0, tiled=True
        ).astype(jnp.float32),
        lax.psum_scatter(
            outer_grad.astype(jnp.bfloat16), "dp", scatter_dimension=0, tiled=True
        ).astype(jnp.float32),
        lax.psum_scatter(
            small_sums[5].astype(jnp.bfloat16), "dp", scatter_dimension=0, tiled=True
        ).astype(jnp.float32),
    )
    return (
        layer_output,
        input_grad,
        everything[0],
        everything[1],
        everything[2],
        everything[3],
        everything[4],
        everything[5],
        everything[6],
        everything[7],
        everything[8],
        everything[9],
        everything[10],
        everything[11],
    )


def solution(mesh):
    in_specs = (
        P(("dp", "tensor"), None),
        P("dp", None),
        P("dp"),
        P("dp"),
        P("dp", "tensor"),
        P(("tensor", "dp")),
        P("dp", "tensor"),
        P("dp"),
        P("dp"),
        P("dp"),
        P("dp", "tensor"),
        P(("tensor", "dp")),
        P("dp", "tensor"),
        P("dp"),
        P(("dp", "tensor"), None),
    )
    out_specs = (
        P(("dp", "tensor"), None),
        P(("dp", "tensor"), None),
        P("dp"),
        P("dp"),
        P("dp", "tensor"),
        P(("tensor", "dp")),
        P("dp", "tensor"),
        P("dp"),
        P("dp"),
        P("dp"),
        P("dp", "tensor"),
        P(("tensor", "dp")),
        P("dp", "tensor"),
        P("dp"),
    )
    return jax.shard_map(
        on_device, mesh=mesh, in_specs=in_specs, out_specs=out_specs, check_vma=False
    )
```

profile of v0, /device:TPU:0, one launch (start us, length us, event | category | flops | bytes accessed | tf_op | source)
XLA Modules:
  0.0 754.2 jit_solution(11036563063567816782)
XLA Ops:
  14.3 63.0 %all-reduce.17 = (bf16[1024]{0:T(1024)(128)(2,1)S(1)}, bf16[1024]{0:T(1024)(128)(2,1)S(1)}, bf16[1024]{0:T(1024)(128)(2,1)S(1)}, bf16[1024]{0:T(1024)(128)(2,1)S...) all-reduce(bf16[1024]{0:T(1024)(128)(2,1)S(1)} %dynamic-update-slic, ...), channel_id=1, replica_groups=mesh['dp'=16,'tensor'=2] {'dp'}, use_global_device_ids=true, to_apply=%add.1 | all-reduce | flops 6144 | bytes 24576
  78.6 1.5 multiply_reduce_fusion.2
  80.1 2.3 add_convert_fusion.1
  84.6 16.5 %all-gather.10.cloned.1.call-done = bf16[512,1024]{1,0:T(8,128)(2,1)} async-done(((bf16[256,1024]{1,0:T(8,128)(2,1)}), bf16[512,1024]{1,0:T(8,128)(2,1)}) %all-gather.10.cloned.1.call-update) | async-done | bytes 1048592 | tf_op jit(solution)/shard_map/all_gather | solution.py:155
  101.1 47.8 %all-gather.12.cloned.1.call-done = bf16[1024,1536]{1,0:T(8,128)(2,1)} async-done(((bf16[64,1536]{1,0:T(8,128)(2,1)}), bf16[1024,1536]{1,0:T(8,128)(2,1)}) %all-gather.12.cloned.1.call-update) | async-done | bytes 3145744 | tf_op jit(solution)/shard_map/all_gather | solution.py:121
  148.9 5.2 fusion.9
  154.0 1.7 copy.60
  155.8 2.4 fusion.42
  159.4 2.0 copy-done
  161.4 1.4 convolution_convert_fusion.7
  162.9 24.4 %all-gather.14.cloned.1.call-done = bf16[1024,512]{1,0:T(8,128)(2,1)} async-done(((bf16[64,512]{1,0:T(8,128)(2,1)}), bf16[1024,512]{1,0:T(8,128)(2,1)}) %all-gather.14.cloned.1.call-update) | async-done | bytes 1048592 | tf_op jit(solution)/shard_map/all_gather | solution.py:123
  187.3 3.0 convolution_convert_fusion.4
  191.0 18.8 %reduce-scatter.11.cloned.1.call-done = bf16[256,1024]{1,0:T(8,128)(2,1)} async-done(((bf16[512,1024]{1,0:T(8,128)(2,1)}), bf16[256,1024]{1,0:T(8,128)(2,1)}) %reduce-scatter.11.cloned.1.call-update) | async-done | bytes 524304 | tf_op jit(solution)/shard_map/reduce_scatter | solution.py:166
  214.2 22.0 %all-gather = bf16[16,1,128]{2,1,0:T(2,128)(2,1)S(1)} all-gather(bf16[1,1,128]{2,1,0:T(2,128)(2,1)S(1)} %bitcast.96), channel_id=1, replica_groups=mesh['dp'=16,'tensor'=2] {'dp'}, dimensions={0}, use_global_device_ids=true | all-gather | bytes 4352 | tf_op jit(solution)/shard_map/all_gather | solution.py:128
  236.2 26.1 %all-gather.18.cloned.1.call-done = bf16[1024,2048]{1,0:T(8,128)(2,1)} async-done(((bf16[64,2048]{1,0:T(8,128)(2,1)}), bf16[1024,2048]{1,0:T(8,128)(2,1)}) %all-gather.18.cloned.1.call-update) | async-done | bytes 4194320 | tf_op jit(solution)/shard_map/all_gather | solution.py:127
  262.3 21.8 %all-gather.16.cloned.1.call-done = bf16[512,1024]{1,0:T(8,128)(2,1)} async-done(((bf16[256,1024]{1,0:T(8,128)(2,1)}), bf16[512,1024]{1,0:T(8,128)(2,1)}) %all-gather.16.cloned.1.call-update) | async-done | bytes 1048592 | tf_op jit(solution)/shard_map/all_gather | solution.py:174
  284.1 6.8 fusion.44
  290.9 16.6 %all-gather.22.cloned.1.call-done = bf16[512,1024]{1,0:T(8,128)(2,1)} async-done(((bf16[256,1024]{1,0:T(8,128)(2,1)}), bf16[512,1024]{1,0:T(8,128)(2,1)}) %all-gather.22.cloned.1.call-update) | async-done | bytes 1048592 | tf_op jit(solution)/shard_map/all_gather | solution.py:199
  307.5 52.6 %all-gather.20.cloned.1.call-done = bf16[1024,2048]{1,0:T(8,128)(2,1)} async-done(((bf16[64,2048]{1,0:T(8,128)(2,1)}), bf16[1024,2048]{1,0:T(8,128)(2,1)}) %all-gather.20.cloned.1.call-update) | async-done | bytes 4194320 | tf_op jit(solution)/shard_map/all_gather | solution.py:129
  360.1 8.4 %fusion.43 = (bf16[2048]{0:T(1024)(128)(2,1)S(1)}, bf16[512,2048]{1,0:T(8,128)(2,1)S(1)}) fusion(f32[512,2048]{1,0:T(8,128)} %fusion.44, f32[2048]{0:T(1024)S(1)} %bitcast.93, bf16[512,1024]{1,0:T(8,128)(2,1)} %all-gather.22.cloned.1.call-done, bf16[1024,2048]{1,0:T(8,128)(2,1)} %all-gather.20.cloned.1.call-done), kind=kOutput, calls=%fused_computation.102 | convolution fusion | flops 2169501696 | bytes 11546624 | tf_op jit(solution)/shard_map/dot_general | solution.py:201
  369.9 3.3 convolution_convert_fusion.5
  373.3 19.0 %reduce-scatter.15.cloned.1.call-done = bf16[256,1024]{1,0:T(8,128)(2,1)} async-done(((bf16[512,1024]{1,0:T(8,128)(2,1)}), bf16[256,1024]{1,0:T(8,128)(2,1)}) %reduce-scatter.15.cloned.1.call-update) | async-done | bytes 524304 | tf_op jit(solution)/shard_map/reduce_scatter | solution.py:205
  392.3 1.6 fusion.30
  393.9 1.8 fusion.35
  396.6 21.4 %all-gather.24.cloned.1.call-done = bf16[512,1024]{1,0:T(8,128)(2,1)} async-done(((bf16[256,1024]{1,0:T(8,128)(2,1)}), bf16[512,1024]{1,0:T(8,128)(2,1)}) %all-gather.24.cloned.1.call-update) | async-done | bytes 1048592 | tf_op jit(solution)/shard_map/all_gather | solution.py:216
  418.0 3.1 convolution_convert_fusion.3
  421.3 2.6 multiply_reduce_fusion
  424.0 4.9 multiply_convert_fusion
  436.0 2.8 convolution_convert_fusion.2
  438.9 7.3 convolution_convert_fusion.6
  446.4 7.9 %convert_bitcast_fusion = bf16[1024,2048]{0,1:T(8,128)(2,1)} fusion(bf16[512,1024]{1,0:T(8,128)(2,1)} %all-gather.22.cloned.1.call-done, f32[512,2048]{1,0:T(8,128)} %fusion.44, f32[2048]{0:T(1024)S(1)} %bitcast.95), kind=kOutput, calls=%fused_computation.15 | convolution fusion | flops 2160066560 | bytes 9445376 | tf_op jit(solution)/shard_map/dot_general | solution.py:40
  454.3 6.5 copy.77
  460.9 6.3 convolution_convert_fusion
  467.3 5.3 convolution_convert_fusion.1
  474.2 2.2 fusion.10
  476.5 2.9 reduce-scatter.21.cloned.1.call-done
  479.4 1.5 convert_element_type.230
  480.9 20.5 %reduce-scatter.17.cloned.1.call-done = bf16[256,1024]{1,0:T(8,128)(2,1)} async-done(((bf16[512,1024]{1,0:T(8,128)(2,1)}), bf16[256,1024]{1,0:T(8,128)(2,1)}) %reduce-scatter.17.cloned.1.call-update) | async-done | bytes 524304 | tf_op jit(solution)/shard_map/reduce_scatter | solution.py:232
  501.4 1.6 fusion.31
  503.0 7.1 all-reduce.15
  510.1 60.0 %all-reduce.16 = (bf16[1024]{0:T(1024)(128)(2,1)S(1)}, bf16[1024]{0:T(1024)(128)(2,1)S(1)}, bf16[1024]{0:T(1024)(128)(2,1)S(1)}, bf16[1024]{0:T(1024)(128)(2,1)S...) all-reduce(bf16[1024]{0:T(1024)(128)(2,1)S(1)} %dynamic-update-slic, ...), channel_id=1, replica_groups=mesh['dp'=16,'tensor'=2] {'dp'}, use_global_device_ids=true, to_apply=%add.6 | all-reduce | flops 10240 | bytes 40960
  574.8 2.2 add_add_fusion
  577.0 2.4 fusion.24
  579.4 21.6 %reduce-scatter.25.cloned.1.call-done = bf16[64,2048]{1,0:T(8,128)(2,1)} async-done(((bf16[1024,2048]{1,0:T(8,128)(2,1)}), bf16[64,2048]{1,0:T(8,128)(2,1)}) %reduce-scatter.25.cloned.1.call-update) | async-done | bytes 262160
  603.2 73.4 %reduce-scatter.23.cloned.1.call-done = bf16[64,2048]{1,0:T(8,128)(2,1)} async-done(((bf16[1024,2048]{1,0:T(8,128)(2,1)}), bf16[64,2048]{1,0:T(8,128)(2,1)}) %reduce-scatter.23.cloned.1.call-update) | async-done | bytes 262160 | tf_op jit(solution)/shard_map/reduce_scatter | solution.py:277
  676.6 1.8 convert_element_type.238
  678.4 67.3 %reduce-scatter.19.cloned.1.call-done = bf16[64,1536]{1,0:T(8,128)(2,1)} async-done(((bf16[1024,1536]{1,0:T(8,128)(2,1)}), bf16[64,1536]{1,0:T(8,128)(2,1)}) %reduce-scatter.19.cloned.1.call-update) | async-done | bytes 196624 | tf_op jit(solution)/shard_map/reduce_scatter | solution.py:259
  745.7 1.7 convert_element_type.226
  (133 shorter events, 33.5 us)
Async XLA Ops:
  7.2 77.2 %copy-start.10 = (s32[1,512]{1,0:T(1,128)S(1)}, s32[1,512]{1,0:T(1,128)}, u32[]{:S(2)}) copy-start(s32[1,512]{1,0:T(1,128)} %param.16) | copy-start | bytes 6148
  7.2 93.9 %all-gather.10.cloned.1.call-start = ((), (), s32[]{:S(2)}) async-start(), calls=%async_computation.8 | async-start | bytes 1572864 | tf_op jit(solution)/shard_map/all_gather | solution.py:155
  82.4 66.4 %all-gather.12.cloned.1.call-start = ((), (), s32[]{:S(2)}) async-start(), calls=%async_computation.9 | async-start | bytes 3342336 | tf_op jit(solution)/shard_map/all_gather | solution.py:121
  83.2 104.2 %all-gather.14.cloned.1.call-start = ((), (), s32[]{:S(2)}) async-start(), calls=%async_computation.10 | async-start | bytes 1114112 | tf_op jit(solution)/shard_map/all_gather | solution.py:123
  83.9 125.9 %reduce-scatter.11.cloned.1.call-start = ((), (), s32[]{:S(2)}) async-start(), calls=%async_computation.11 | async-start | bytes 1572864 | tf_op jit(solution)/shard_map/reduce_scatter | solution.py:166
  155.7 3.7 copy-start.5
  158.2 3.2 copy-start
  162.8 28.1 %copy-start.9 = (bf16[8,64,512]{2,1,0:T(8,128)(2,1)}, bf16[8,64,512]{2,1,0:T(8,128)(2,1)S(1)}, u32[]{:S(2)}) copy-start(bf16[8,64,512]{2,1,0:T(8,128)(2,1)S(1)} %convolution_convert_fusion.7) | copy-start | bytes 1572868
  162.9 46.9 %copy-start.1 = (f32[256,1024]{1,0:T(8,128)S(1)}, f32[256,1024]{1,0:T(8,128)}, u32[]{:S(2)}) copy-start(f32[256,1024]{1,0:T(8,128)} %param.15) | copy-start | bytes 3145732
  190.3 22.2 %copy-start.7 = (f32[256,1024]{1,0:T(8,128)S(1)}, f32[256,1024]{1,0:T(8,128)}, u32[]{:S(2)}) copy-start(f32[256,1024]{1,0:T(8,128)} %param.29) | copy-start | bytes 3145732
  190.3 23.9 %copy-start.11 = (bf16[128]{0:T(256)(128)(2,1)S(1)}, bf16[128]{0:T(256)(128)(2,1)}, u32[]{:S(2)}) copy-start(bf16[128]{0:T(256)(128)(2,1)} %param.26) | copy-start | bytes 772
  190.3 72.0 %all-gather.18.cloned.1.call-start = ((), (), s32[]{:S(2)}) async-start(), calls=%async_computation.13 | async-start | bytes 4456448 | tf_op jit(solution)/shard_map/all_gather | solution.py:127
  190.9 93.2 %all-gather.16.cloned.1.call-start = ((), (), s32[]{:S(2)}) async-start(), calls=%async_computation.12 | async-start | bytes 1572864 | tf_op jit(solution)/shard_map/all_gather | solution.py:174
  212.4 95.1 %all-gather.22.cloned.1.call-start = ((), (), s32[]{:S(2)}) async-start(), calls=%async_computation.16 | async-start | bytes 1572864 | tf_op jit(solution)/shard_map/all_gather | solution.py:199
  213.4 146.7 %all-gather.20.cloned.1.call-start = ((), (), s32[]{:S(2)}) async-start(), calls=%async_computation.14 | async-start | bytes 4456448 | tf_op jit(solution)/shard_map/all_gather | solution.py:129
  214.1 178.2 %reduce-scatter.15.cloned.1.call-start = ((), (), s32[]{:S(2)}) async-start(), calls=%async_computation.17 | async-start | bytes 1572864 | tf_op jit(solution)/shard_map/reduce_scatter | solution.py:205
  360.1 9.8 %copy-start.12 = (bf16[1024,2048]{1,0:T(8,128)(2,1)S(1)}, bf16[1024,2048]{1,0:T(8,128)(2,1)}, u32[]{:S(2)}) copy-start(bf16[1024,2048]{1,0:T(8,128)(2,1)} %all-gather.18.cloned.1.call-done) | copy-start | bytes 12582916
  368.5 1.4 copy-start.15
  373.3 44.8 %all-gather.24.cloned.1.call-start = ((), (), s32[]{:S(2)}) async-start(), calls=%async_computation.18 | async-start | bytes 1572864 | tf_op jit(solution)/shard_map/all_gather | solution.py:216
  396.6 82.8 %reduce-scatter.21.cloned.1.call-start = ((), (), s32[]{:S(2)}) async-start(), calls=%async_computation.21 | async-start | bytes 1114112 | tf_op jit(solution)/shard_map/reduce_scatter | solution.py:265
  421.1 80.3 %reduce-scatter.17.cloned.1.call-start = ((), (), s32[]{:S(2)}) async-start(), calls=%async_computation.19 | async-start | bytes 1572864 | tf_op jit(solution)/shard_map/reduce_scatter | solution.py:232
  421.3 9.7 %slice-start = ((s8[8388608]{0:T(1024)(128)(4,1)}), s8[4194304]{0:T(1024)(128)(4,1)S(1)}, s32[]{:S(2)}) async-start(s8[8388608]{0:T(1024)(128)(4,1)} %bitcast.78), calls=%async_computation.24 | async-start | bytes 8388608
  424.0 4.9 copy-start.6
  424.0 7.1 slice-start.1
  430.3 2.2 copy-start.3
  431.1 1.4 copy-start.4
  432.5 1.0 copy-start.2
  433.5 2.5 copy-start.13
  434.0 1.2 copy-start.8
  438.9 135.9 %reduce-scatter.13.cloned.1.call-start = ((), (), s32[]{:S(2)}) async-start(), calls=%async_computation.15 | async-start | bytes 1572864 | tf_op jit(solution)/shard_map/reduce_scatter | solution.py:182
  446.2 154.8 %reduce-scatter.25.cloned.1.call-start = ((), (), s32[]{:S(2)}) async-start(), calls=%async_computation.23 | async-start | bytes 4456448
  460.8 215.8 %reduce-scatter.23.cloned.1.call-start = ((), (), s32[]{:S(2)}) async-start(), calls=%async_computation.22 | async-start | bytes 4456448 | tf_op jit(solution)/shard_map/reduce_scatter | solution.py:277
  467.2 6.7 copy-start.14
  467.2 278.5 %reduce-scatter.19.cloned.1.call-start = ((), (), s32[]{:S(2)}) async-start(), calls=%async_computation.20 | async-start | bytes 3342336 | tf_op jit(solution)/shard_map/reduce_scatter | solution.py:259
Sparse Core Ops, SparseCore 0:
  82.5 18.5 all-gather.9
  103.4 45.4 all-gather.11
  151.0 36.2 all-gather.13
  190.4 19.3 reduce-scatter.10
  211.8 50.4 all-gather.17
  264.3 19.7 all-gather.15
  286.2 21.2 all-gather.21
  309.7 50.3 all-gather.19
  373.4 18.9 reduce-scatter.14
  396.7 21.2 all-gather.23
  421.6 57.6 reduce-scatter.20
  482.0 19.3 reduce-scatter.16
  504.2 20.3 reduce-scatter.12
  528.4 72.6 reduce-scatter.24
  604.7 71.8 reduce-scatter.22
  680.3 65.3 reduce-scatter.18
where the time goes:
time: 763 us; the launch traced here: 754 us
  waiting for transfers between devices  454 us (60%)
  blocking collectives  152 us (20%)
  matrix products  74.2 us (10%)
  other arithmetic  32.8 us (4%)
  local copies, waits for them, and re-layouts  23.9 us (3%)
  between operations  16.6 us (2%)
    unnamed x2, blocking collectives  123 us
    reduce_scatter x1, waiting for transfers between devices, on_device(): lax.psum_scatter(inner_grad.astype(jnp.bfloat16), 'dp', scatter_dimension...  73.4 us
    reduce_scatter x1, waiting for transfers between devices, on_device(): lax.psum_scatter(qkv_weight_grad.astype(jnp.bfloat16), 'dp', scatter_dime...  67.3 us
    all_gather x1, waiting for transfers between devices, on_device(): lax.all_gather(outer_weight, 'dp', axis=0, tiled=True)  52.6 us
    all_gather x1, waiting for transfers between devices, on_device(): lax.all_gather(qkv_weight, 'dp', axis=0, tiled=True)  47.8 us
    all_gather x1, waiting for transfers between devices, on_device(): lax.all_gather(inner_weight, 'dp', axis=0, tiled=True)  26.1 us
    unnamed x17, waiting for transfers between devices  24.5 us
    all_gather x1, waiting for transfers between devices, on_device(): lax.all_gather(dense_weight, 'dp', axis=0, tiled=True)  24.4 us
  transfers between devices with their start and end apart: 16, of which 15 were waited for; matrix products, arithmetic and copies ran while one was open for 12% of the time, Pallas kernels for 0%

commit v1 on v0

--- a/solution.py
+++ b/solution.py
@@ -118,7 +118,9 @@
     gathered = (
         lax.all_gather(norm1_gain, "dp", axis=0, tiled=True),
         lax.all_gather(norm1_shift, "dp", axis=0, tiled=True),
-        lax.all_gather(qkv_weight, "dp", axis=0, tiled=True),
+        jnp.concatenate(
+            lax.all_to_all(jnp.stack([qkv_weight] * lax.axis_size("dp")), "dp", 0, 0), axis=0
+        ),
         lax.all_gather(qkv_bias, "dp", axis=0, tiled=True),
         lax.all_gather(dense_weight, "dp", axis=0, tiled=True),
         lax.all_gather(dense_bias, "dp", axis=0, tiled=True),

time: 763 us -> 811 us (1.063)
  blocking collectives: 152 us -> 195 us
  matrix products: 74.2 us -> 87.8 us
  waiting for transfers between devices: 454 us -> 441 us
    unnamed x2, blocking collectives: 123 us -> 166 us
    all_gather x1, waiting for transfers between devices: 47.8 us -> 20.8 us  [on_device(): lax.all_gather(qkv_weight, 'dp', axis=0, tiled=True)]
    reduce_scatter x1, waiting for transfers between devices: 2.91 us -> 16.7 us  [on_device(): lax.psum_scatter(dense_grad.astype(jnp.bfloat16), 'dp', scatter_dimension...]
    unnamed x54 -> x62, local copies, waits for them, and re-layouts: 21.7 us -> 16.2 us
  transfers between devices with their start and end apart: 16 -> 17, of which waited for: 15 -> 15; matrix products, arithmetic and copies ran while one was open for 12% -> 14% of each run, Pallas kernels for 0% -> 0%
where the time goes in v1:
time: 811 us; the launch traced here: 802 us
  waiting for transfers between devices  441 us (54%)
  blocking collectives  195 us (24%)
  matrix products  87.8 us (11%)
  other arithmetic  29.1 us (4%)
  local copies, waits for them, and re-layouts  23.5 us (3%)
  between operations  16.6 us (2%)
  starting transfers between devices  8.49 us (1%)
    unnamed x2, blocking collectives  166 us
    reduce_scatter x1, waiting for transfers between devices, on_device(): lax.psum_scatter(inner_grad.astype(jnp.bfloat16), 'dp', scatter_dimension...  73.3 us
    reduce_scatter x1, waiting for transfers between devices, on_device(): lax.psum_scatter(qkv_weight_grad.astype(jnp.bfloat16), 'dp', scatter_dime...  67.3 us
    all_gather x1, waiting for transfers between devices, on_device(): lax.all_gather(outer_weight, 'dp', axis=0, tiled=True)  52.6 us
    all_gather x1, waiting for transfers between devices, on_device(): lax.all_gather(inner_weight, 'dp', axis=0, tiled=True)  26.1 us
    unnamed x17, waiting for transfers between devices  24.4 us
    all_gather x1, waiting for transfers between devices, on_device(): lax.all_gather(dense_weight, 'dp', axis=0, tiled=True)  22.9 us
    dot_general x4, matrix products, rows_product(): lax.dot_general(left, right, (((0,), (0,)), ((), ())), preferred_element_...  22.6 us
  transfers between devices with their start and end apart: 17, of which 15 were waited for; matrix products, arithmetic and copies ran while one was open for 14% of the time, Pallas kernels for 0%

profile of v1, /device:TPU:0, one launch (start us, length us, event | category | flops | bytes accessed | tf_op | source)
XLA Modules:
  0.0 801.9 jit_solution(17110040245635885036)
XLA Ops:
  7.3 3.0 stack.15
  10.3 7.5 all-to-all-start
  20.5 106.3 %all-reduce.17 = (bf16[1024]{0:T(1024)(128)(2,1)S(1)}, bf16[1024]{0:T(1024)(128)(2,1)S(1)}, bf16[1024]{0:T(1024)(128)(2,1)S(1)}, bf16[1024]{0:T(1024)(128)(2,1)S...) all-reduce(bf16[1024]{0:T(1024)(128)(2,1)S(1)} %dynamic-update-slic, ...), channel_id=1, replica_groups=mesh['dp'=16,'tensor'=2] {'dp'}, use_global_device_ids=true, to_apply=%add.1 | all-reduce | flops 6144 | bytes 24576
  129.8 19.5 %all-gather.10.cloned.1.call-done = bf16[512,1024]{1,0:T(8,128)(2,1)} async-done(((bf16[256,1024]{1,0:T(8,128)(2,1)}), bf16[512,1024]{1,0:T(8,128)(2,1)}) %all-gather.10.cloned.1.call-update) | async-done | bytes 1048592 | tf_op jit(solution)/shard_map/all_gather | solution.py:157
  149.3 5.1 fusion.9
  154.4 2.6 copy.60
  157.1 3.7 fusion.42
  162.0 2.0 copy-done
  164.0 2.5 convolution_convert_fusion.7
  166.5 22.9 %all-gather.12.cloned.1.call-done = bf16[1024,512]{1,0:T(8,128)(2,1)} async-done(((bf16[64,512]{1,0:T(8,128)(2,1)}), bf16[1024,512]{1,0:T(8,128)(2,1)}) %all-gather.12.cloned.1.call-update) | async-done | bytes 1048592 | tf_op jit(solution)/shard_map/all_gather | solution.py:125
  189.3 3.0 convolution_convert_fusion.4
  193.0 18.8 %reduce-scatter.11.cloned.1.call-done = bf16[256,1024]{1,0:T(8,128)(2,1)} async-done(((bf16[512,1024]{1,0:T(8,128)(2,1)}), bf16[256,1024]{1,0:T(8,128)(2,1)}) %reduce-scatter.11.cloned.1.call-update) | async-done | bytes 524304 | tf_op jit(solution)/shard_map/reduce_scatter | solution.py:168
  216.2 22.0 %all-gather = bf16[16,1,128]{2,1,0:T(2,128)(2,1)S(1)} all-gather(bf16[1,1,128]{2,1,0:T(2,128)(2,1)S(1)} %bitcast.95), channel_id=1, replica_groups=mesh['dp'=16,'tensor'=2] {'dp'}, dimensions={0}, use_global_device_ids=true | all-gather | bytes 4352 | tf_op jit(solution)/shard_map/all_gather | solution.py:130
  238.2 26.1 %all-gather.16.cloned.1.call-done = bf16[1024,2048]{1,0:T(8,128)(2,1)} async-done(((bf16[64,2048]{1,0:T(8,128)(2,1)}), bf16[1024,2048]{1,0:T(8,128)(2,1)}) %all-gather.16.cloned.1.call-update) | async-done | bytes 4194320 | tf_op jit(solution)/shard_map/all_gather | solution.py:129
  264.3 21.8 %all-gather.14.cloned.1.call-done = bf16[512,1024]{1,0:T(8,128)(2,1)} async-done(((bf16[256,1024]{1,0:T(8,128)(2,1)}), bf16[512,1024]{1,0:T(8,128)(2,1)}) %all-gather.14.cloned.1.call-update) | async-done | bytes 1048592 | tf_op jit(solution)/shard_map/all_gather | solution.py:176
  286.1 6.8 fusion.44
  293.0 16.5 %all-gather.20.cloned.1.call-done = bf16[512,1024]{1,0:T(8,128)(2,1)} async-done(((bf16[256,1024]{1,0:T(8,128)(2,1)}), bf16[512,1024]{1,0:T(8,128)(2,1)}) %all-gather.20.cloned.1.call-update) | async-done | bytes 1048592 | tf_op jit(solution)/shard_map/all_gather | solution.py:201
  309.4 52.6 %all-gather.18.cloned.1.call-done = bf16[1024,2048]{1,0:T(8,128)(2,1)} async-done(((bf16[64,2048]{1,0:T(8,128)(2,1)}), bf16[1024,2048]{1,0:T(8,128)(2,1)}) %all-gather.18.cloned.1.call-update) | async-done | bytes 4194320 | tf_op jit(solution)/shard_map/all_gather | solution.py:131
  362.0 8.4 %fusion.43 = (bf16[2048]{0:T(1024)(128)(2,1)S(1)}, bf16[512,2048]{1,0:T(8,128)(2,1)S(1)}) fusion(f32[512,2048]{1,0:T(8,128)} %fusion.44, f32[2048]{0:T(1024)S(1)} %bitcast.92, bf16[512,1024]{1,0:T(8,128)(2,1)} %all-gather.20.cloned.1.call-done, bf16[1024,2048]{1,0:T(8,128)(2,1)} %all-gather.18.cloned.1.call-done), kind=kOutput, calls=%fused_computation.102 | convolution fusion | flops 2169501696 | bytes 11546624 | tf_op jit(solution)/shard_map/dot_general | solution.py:203
  371.8 3.3 convolution_convert_fusion.5
  375.2 19.0 %reduce-scatter.15.cloned.1.call-done = bf16[256,1024]{1,0:T(8,128)(2,1)} async-done(((bf16[512,1024]{1,0:T(8,128)(2,1)}), bf16[256,1024]{1,0:T(8,128)(2,1)}) %reduce-scatter.15.cloned.1.call-update) | async-done | bytes 524304 | tf_op jit(solution)/shard_map/reduce_scatter | solution.py:207
  395.8 1.8 fusion.35
  399.1 20.8 %all-gather.22.cloned.1.call-done = bf16[512,1024]{1,0:T(8,128)(2,1)} async-done(((bf16[256,1024]{1,0:T(8,128)(2,1)}), bf16[512,1024]{1,0:T(8,128)(2,1)}) %all-gather.22.cloned.1.call-update) | async-done | bytes 1048592 | tf_op jit(solution)/shard_map/all_gather | solution.py:218
  419.9 3.1 convolution_convert_fusion.3
  423.0 2.5 multiply_reduce_fusion
  426.3 6.1 multiply_convert_fusion
  432.6 3.9 fusion.18
  436.6 2.2 fusion.19
  438.8 5.2 convolution_bitcast_fusion
  446.7 20.8 %all-gather.24.cloned.1.call-done = bf16[1024,1536]{1,0:T(8,128)(2,1)} async-done(((bf16[64,1536]{1,0:T(8,128)(2,1)}), bf16[1024,1536]{1,0:T(8,128)(2,1)}) %all-gather.24.cloned.1.call-update) | async-done | bytes 3145744 | tf_op jit(solution)/shard_map/all_gather | solution.py:194
  467.5 5.2 convolution_convert_fusion.2
  472.8 7.3 convolution_convert_fusion.6
  480.1 7.8 convert_bitcast_fusion
  488.0 6.5 copy.77
  494.7 6.3 convolution_convert_fusion
  501.1 5.4 convolution_convert_fusion.1
  508.1 2.2 fusion.10
  510.3 16.7 %reduce-scatter.21.cloned.1.call-done = bf16[64,512]{1,0:T(8,128)(2,1)} async-done(((bf16[1024,512]{1,0:T(8,128)(2,1)}), bf16[64,512]{1,0:T(8,128)(2,1)}) %reduce-scatter.21.cloned.1.call-update) | async-done | bytes 65552 | tf_op jit(solution)/shard_map/reduce_scatter | solution.py:267
  528.6 20.6 %reduce-scatter.17.cloned.1.call-done = bf16[256,1024]{1,0:T(8,128)(2,1)} async-done(((bf16[512,1024]{1,0:T(8,128)(2,1)}), bf16[256,1024]{1,0:T(8,128)(2,1)}) %reduce-scatter.17.cloned.1.call-update) | async-done | bytes 524304 | tf_op jit(solution)/shard_map/reduce_scatter | solution.py:234
  550.8 7.1 all-reduce.15
  557.9 60.0 %all-reduce.16 = (bf16[1024]{0:T(1024)(128)(2,1)S(1)}, bf16[1024]{0:T(1024)(128)(2,1)S(1)}, bf16[1024]{0:T(1024)(128)(2,1)S(1)}, bf16[1024]{0:T(1024)(128)(2,1)S...) all-reduce(bf16[1024]{0:T(1024)(128)(2,1)S(1)} %dynamic-update-slic, ...), channel_id=1, replica_groups=mesh['dp'=16,'tensor'=2] {'dp'}, use_global_device_ids=true, to_apply=%add.6 | all-reduce | flops 10240 | bytes 40960
  622.6 2.2 add_add_fusion
  624.8 2.4 fusion.24
  627.2 21.7 %reduce-scatter.25.cloned.1.call-done = bf16[64,2048]{1,0:T(8,128)(2,1)} async-done(((bf16[1024,2048]{1,0:T(8,128)(2,1)}), bf16[64,2048]{1,0:T(8,128)(2,1)}) %reduce-scatter.25.cloned.1.call-update) | async-done | bytes 262160
  651.1 73.3 %reduce-scatter.23.cloned.1.call-done = bf16[64,2048]{1,0:T(8,128)(2,1)} async-done(((bf16[1024,2048]{1,0:T(8,128)(2,1)}), bf16[64,2048]{1,0:T(8,128)(2,1)}) %reduce-scatter.23.cloned.1.call-update) | async-done | bytes 262160 | tf_op jit(solution)/shard_map/reduce_scatter | solution.py:279
  724.4 1.8 convert_element_type.238
  726.2 67.3 %reduce-scatter.19.cloned.1.call-done = bf16[64,1536]{1,0:T(8,128)(2,1)} async-done(((bf16[1024,1536]{1,0:T(8,128)(2,1)}), bf16[64,1536]{1,0:T(8,128)(2,1)}) %reduce-scatter.19.cloned.1.call-update) | async-done | bytes 196624 | tf_op jit(solution)/shard_map/reduce_scatter | solution.py:261
  793.5 1.7 convert_element_type.226
  (143 shorter events, 30.1 us)
Async XLA Ops:
  7.2 10.6 %copy-start.11 = (u32[32]{0:T(128)S(1)}, u32[32]{0:T(128)}, u32[]{:S(2)}) copy-start(u32[32]{0:T(128)} %constant.49) | copy-start | bytes 388
  7.2 11.9 %copy-start.14 = (bf16[64]{0:T(256)(128)(2,1)S(1)}, bf16[64]{0:T(256)(128)(2,1)}, u32[]{:S(2)}) copy-start(bf16[64]{0:T(256)(128)(2,1)} %param.18) | copy-start | bytes 388
  7.2 12.1 %copy-start.15 = (bf16[64]{0:T(256)(128)(2,1)S(1)}, bf16[64]{0:T(256)(128)(2,1)}, u32[]{:S(2)}) copy-start(bf16[64]{0:T(256)(128)(2,1)} %param.17) | copy-start | bytes 388
  7.2 12.4 %copy-start.16 = (bf16[64]{0:T(256)(128)(2,1)S(1)}, bf16[64]{0:T(256)(128)(2,1)}, u32[]{:S(2)}) copy-start(bf16[64]{0:T(256)(128)(2,1)} %param.20) | copy-start | bytes 388
  7.2 12.6 %copy-start.17 = (bf16[64]{0:T(256)(128)(2,1)S(1)}, bf16[64]{0:T(256)(128)(2,1)}, u32[]{:S(2)}) copy-start(bf16[64]{0:T(256)(128)(2,1)} %param.22) | copy-start | bytes 388
  7.2 12.8 %copy-start.18 = (bf16[64]{0:T(256)(128)(2,1)S(1)}, bf16[64]{0:T(256)(128)(2,1)}, u32[]{:S(2)}) copy-start(bf16[64]{0:T(256)(128)(2,1)} %param.24) | copy-start | bytes 388
  7.2 13.0 %copy-start.19 = (bf16[64]{0:T(256)(128)(2,1)S(1)}, bf16[64]{0:T(256)(128)(2,1)}, u32[]{:S(2)}) copy-start(bf16[64]{0:T(256)(128)(2,1)} %param.23) | copy-start | bytes 388
  7.3 119.5 %copy-start.1 = (f32[256,1024]{1,0:T(8,128)S(1)}, f32[256,1024]{1,0:T(8,128)}, u32[]{:S(2)}) copy-start(f32[256,1024]{1,0:T(8,128)} %param.15) | copy-start | bytes 3145732
  10.3 139.0 %all-to-all-start = ((bf16[16,64,1536]{2,1,0:T(8,128)(2,1)}), bf16[16,64,1536]{2,1,0:T(8,128)(2,1)}, u32[]{:S(2)}, u32[]{:S(2)}) async-start(bf16[16,64,1536]{2,1,0:T(8,128)(2,1)} %stack.15), calls=%async_computation | async-start | bytes 6291456 | tf_op jit(solution)/shard_map/all_to_all | solution.py:122
  17.8 111.8 %copy-start.10 = (s32[1,512]{1,0:T(1,128)S(1)}, s32[1,512]{1,0:T(1,128)}, u32[]{:S(2)}) copy-start(s32[1,512]{1,0:T(1,128)} %param.16) | copy-start | bytes 6148
  17.8 131.5 %all-gather.10.cloned.1.call-start = ((), (), s32[]{:S(2)}) async-start(), calls=%async_computation.9 | async-start | bytes 1572864 | tf_op jit(solution)/shard_map/all_gather | solution.py:157
  128.3 61.1 %all-gather.12.cloned.1.call-start = ((), (), s32[]{:S(2)}) async-start(), calls=%async_computation.10 | async-start | bytes 1114112 | tf_op jit(solution)/shard_map/all_gather | solution.py:125
  129.0 82.8 %reduce-scatter.11.cloned.1.call-start = ((), (), s32[]{:S(2)}) async-start(), calls=%async_computation.11 | async-start | bytes 1572864 | tf_op jit(solution)/shard_map/reduce_scatter | solution.py:168
  160.7 3.2 copy-start
  166.4 26.6 %copy-start.9 = (bf16[8,64,512]{2,1,0:T(8,128)(2,1)}, bf16[8,64,512]{2,1,0:T(8,128)(2,1)S(1)}, u32[]{:S(2)}) copy-start(bf16[8,64,512]{2,1,0:T(8,128)(2,1)S(1)} %convolution_convert_fusion.7) | copy-start | bytes 1572868
  192.3 22.2 %copy-start.6 = (f32[256,1024]{1,0:T(8,128)S(1)}, f32[256,1024]{1,0:T(8,128)}, u32[]{:S(2)}) copy-start(f32[256,1024]{1,0:T(8,128)} %param.29) | copy-start | bytes 3145732
  192.3 23.9 %copy-start.12 = (bf16[128]{0:T(256)(128)(2,1)S(1)}, bf16[128]{0:T(256)(128)(2,1)}, u32[]{:S(2)}) copy-start(bf16[128]{0:T(256)(128)(2,1)} %param.26) | copy-start | bytes 772
  192.3 72.0 %all-gather.16.cloned.1.call-start = ((), (), s32[]{:S(2)}) async-start(), calls=%async_computation.13 | async-start | bytes 4456448 | tf_op jit(solution)/shard_map/all_gather | solution.py:129
  192.9 93.2 %all-gather.14.cloned.1.call-start = ((), (), s32[]{:S(2)}) async-start(), calls=%async_computation.12 | async-start | bytes 1572864 | tf_op jit(solution)/shard_map/all_gather | solution.py:176
  214.4 95.0 %all-gather.20.cloned.1.call-start = ((), (), s32[]{:S(2)}) async-start(), calls=%async_computation.16 | async-start | bytes 1572864 | tf_op jit(solution)/shard_map/all_gather | solution.py:201
  215.4 146.6 %all-gather.18.cloned.1.call-start = ((), (), s32[]{:S(2)}) async-start(), calls=%async_computation.14 | async-start | bytes 4456448 | tf_op jit(solution)/shard_map/all_gather | solution.py:131
  216.2 178.1 %reduce-scatter.15.cloned.1.call-start = ((), (), s32[]{:S(2)}) async-start(), calls=%async_computation.17 | async-start | bytes 1572864 | tf_op jit(solution)/shard_map/reduce_scatter | solution.py:207
  362.0 9.8 %copy-start.13 = (bf16[1024,2048]{1,0:T(8,128)(2,1)S(1)}, bf16[1024,2048]{1,0:T(8,128)(2,1)}, u32[]{:S(2)}) copy-start(bf16[1024,2048]{1,0:T(8,128)(2,1)} %all-gather.16.cloned.1.call-done) | copy-start | bytes 12582916
  370.4 1.4 copy-start.21
  375.2 44.8 %all-gather.22.cloned.1.call-start = ((), (), s32[]{:S(2)}) async-start(), calls=%async_computation.18 | async-start | bytes 1572864 | tf_op jit(solution)/shard_map/all_gather | solution.py:218
  398.5 69.0 %all-gather.24.cloned.1.call-start = ((), (), s32[]{:S(2)}) async-start(), calls=%async_computation.19 | async-start | bytes 3342336 | tf_op jit(solution)/shard_map/all_gather | solution.py:194
  399.1 128.0 %reduce-scatter.21.cloned.1.call-start = ((), (), s32[]{:S(2)}) async-start(), calls=%async_computation.22 | async-start | bytes 1114112 | tf_op jit(solution)/shard_map/reduce_scatter | solution.py:267
  425.5 0.8 copy-start.7
  432.4 116.8 %reduce-scatter.17.cloned.1.call-start = ((), (), s32[]{:S(2)}) async-start(), calls=%async_computation.20 | async-start | bytes 1572864 | tf_op jit(solution)/shard_map/reduce_scatter | solution.py:234
  432.6 3.9 copy-start.2
  436.5 7.5 copy-start.4
  436.5 2.2 copy-start.8
  438.8 5.2 copy-start.5
  444.0 1.0 copy-start.3
  472.7 149.8 %reduce-scatter.13.cloned.1.call-start = ((), (), s32[]{:S(2)}) async-start(), calls=%async_computation.15 | async-start | bytes 1572864 | tf_op jit(solution)/shard_map/reduce_scatter | solution.py:184
  480.1 168.8 %reduce-scatter.25.cloned.1.call-start = ((), (), s32[]{:S(2)}) async-start(), calls=%async_computation.24 | async-start | bytes 4456448
  494.5 229.9 %reduce-scatter.23.cloned.1.call-start = ((), (), s32[]{:S(2)}) async-start(), calls=%async_computation.23 | async-start | bytes 4456448 | tf_op jit(solution)/shard_map/reduce_scatter | solution.py:279
  501.1 6.7 copy-start.20
  501.1 292.4 %reduce-scatter.19.cloned.1.call-start = ((), (), s32[]{:S(2)}) async-start(), calls=%async_computation.21 | async-start | bytes 3342336 | tf_op jit(solution)/shard_map/reduce_scatter | solution.py:261
Sparse Core Ops, SparseCore 0:
  128.4 20.8 all-gather.9
  151.4 37.8 all-gather.11
  192.4 19.3 reduce-scatter.10
  213.8 50.4 all-gather.15
  266.3 19.7 all-gather.13
  288.1 21.2 all-gather.19
  311.6 50.3 all-gather.17
  375.3 18.9 reduce-scatter.14
  398.6 21.2 all-gather.21
  422.0 45.4 all-gather.23
  471.1 55.8 reduce-scatter.20
  529.8 19.4 reduce-scatter.16
  552.0 20.3 reduce-scatter.12
  576.2 72.6 reduce-scatter.24
  652.6 71.8 reduce-scatter.22
  728.1 65.3 reduce-scatter.18
